TPU v7x, 32 devices: a whole 2x2x4 slice. The times are simulated.
32 devices in a mesh: items: 16 (over z, y, core), seq: 2 (over x).
Axes of the slice: x: 2, y: 2, z: 4, core: 2. Of those that a mesh axis runs over, the one named last changes fastest.
Arguments:
- frames: bfloat16 [16, 1280, 1024], P('items', 'seq'), may hold values from -6 to 6
- cotangent: bfloat16 [16, 1280, 1024], P('items', 'seq'), may hold values from -6 to 6
- section: int32 [16], P('items'), may hold values from 0 to 7
- prompt_len: int32 [16], P('items'), may hold values from 150 to 600, as said below
- section_embed: float32 [8, 1024], replicated, may hold values from -6 to 6
- ada_proj: bfloat16 [1024, 4096], replicated, may hold values from -0.09375 to 0.09375
- ada_bias: float32 [4096], replicated, may hold values from -4 to 4
- w_qkv: bfloat16 [1024, 3072], replicated, may hold values from -0.1875 to 0.1875
- w_out: bfloat16 [1024, 1024], replicated, may hold values from -3.5 to 3.5
- w_up: bfloat16 [1024, 4096], replicated, may hold values from -0.1875 to 0.1875
- w_down: bfloat16 [4096, 1024], replicated, may hold values from -0.125 to 0.125
Outputs:
- out_frames: bfloat16 [16, 1280, 1024], P('items', 'seq')
- frames_grad: bfloat16 [16, 1280, 1024], P('items', 'seq')
- section_embed_grad: float32 [8, 1024], P(None, 'items')
- ada_proj_grad: float32 [1024, 4096], P('items')
- ada_bias_grad: float32 [4096], P('items')
- w_qkv_grad: float32 [1024, 3072], P('items')
- w_out_grad: float32 [1024, 1024], P('items')
- w_up_grad: float32 [1024, 4096], P('items')
- w_down_grad: float32 [4096, 1024], P('items')
Inputs may be any that keep to these rules, and one draw needn't show every extreme that they name: `prompt_len`: some item has exactly 600 prompt frames.
All inputs are finite; a program needn't handle non-finite values.
Results may differ from a plain program's by a relative error of at most 0.018.
Values may be sent and summed in bfloat16 or wider, within the bound.
A program may use at most 640 MiB of HBM per device.

v0:
```python
import jax
import jax.numpy as jnp
from jax import lax
from jax.sharding import PartitionSpec as P

HEADS = 16
EPS = 1e-05
NEGATIVE = -1e30
SQRT_HALF = 0.7071067811865476
INV_SQRT_TAU = 0.3989422804014327
HIGHEST = lax.Precision.HIGHEST


def normalize(values):
    mean = jnp.mean(values, -1, keepdims=True)
    centered = values - mean
    inverse = lax.rsqrt(jnp.mean(centered * centered, -1, keepdims=True) + EPS)
    return (centered * inverse, inverse)


def norm_back(grad, normed, inverse):
    first = jnp.mean(grad, -1, keepdims=True)
    second = jnp.mean(grad * normed, -1, keepdims=True)
    return (grad - first - normed * second) * inverse


def gelu_exact(values):
    return 0.5 * values * (1.0 + lax.erf(values * SQRT_HALF))


def gelu_slope(values):
    return (
        0.5 * (1.0 + lax.erf(values * SQRT_HALF))
        + values * jnp.exp(-0.5 * values * values) * INV_SQRT_TAU
    )


def project(left, weight):
    flat = left.reshape(-1, left.shape[-1])
    result = jnp.dot(flat, weight, preferred_element_type=jnp.float32)
    return result.reshape(left.shape[:-1] + (weight.shape[1],))


def back_project(grad, weight):
    flat = grad.reshape(-1, grad.shape[-1])
    result = lax.dot_general(
        flat, weight, (((1,), (1,)), ((), ())), preferred_element_type=jnp.float32
    )
    return result.reshape(grad.shape[:-1] + (weight.shape[0],))


def outer_sum(left, right):
    left_flat = left.reshape(-1, left.shape[-1])
    right_flat = right.reshape(-1, right.shape[-1])
    return lax.dot_general(
        left_flat, right_flat, (((0,), (0,)), ((), ())), preferred_element_type=jnp.float32
    )


def per_device(
    frames,
    cotangent,
    section,
    prompt_len,
    section_embed,
    ada_proj,
    ada_bias,
    w_qkv,
    w_out,
    w_up,
    w_down,
):
    group_count, row_count, width = frames.shape
    head_count = HEADS
    head_size = width // head_count
    scale = head_size ** (-0.5)
    section_count = section_embed.shape[0]
    onehot = (section[:, None] == jnp.arange(section_count, dtype=jnp.int32)[None, :]).astype(
        jnp.float32
    )
    cond = jnp.dot(onehot, section_embed, precision=HIGHEST)
    ada_full = ada_proj.astype(jnp.float32)
    modul = jnp.dot(cond, ada_full, precision=HIGHEST) + ada_bias[None, :]
    scale_one, shift_one, scale_two, shift_two = jnp.split(modul, 4, axis=-1)
    inputs = frames.astype(jnp.float32)
    normed_one, inv_one = normalize(inputs)
    attn_in = (normed_one * (1.0 + scale_one[:, None, :]) + shift_one[:, None, :]).astype(
        jnp.bfloat16
    )
    qkv = project(attn_in, w_qkv)
    query = qkv[..., :width].astype(jnp.bfloat16)
    key_local = qkv[..., width : 2 * width].astype(jnp.bfloat16)
    value_local = qkv[..., 2 * width :].astype(jnp.bfloat16)
    query_heads = query.reshape(group_count, row_count, head_count, head_size)

    def key_mask(count):
        position = jnp.arange(count, dtype=jnp.int32)
        valid = (position[None, :] >= row_count) | (position[None, :] < prompt_len[:, None])
        return valid[:, None, None, :]

    run_max = jnp.full((group_count, head_count, row_count), NEGATIVE, jnp.float32)
    key_piece = lax.all_gather(key_local, "seq", axis=1, tiled=True)
    value_piece = lax.all_gather(value_local, "seq", axis=1, tiled=True)
    count = key_piece.shape[1]
    key_heads = key_piece.reshape(group_count, count, head_count, head_size)
    value_heads = value_piece.reshape(group_count, count, head_count, head_size)
    valid = key_mask(count)
    scores = (
        jnp.einsum("grhd,gkhd->ghrk", query_heads, key_heads, preferred_element_type=jnp.float32)
        * scale
    )
    scores = jnp.where(valid, scores, NEGATIVE)
    new_max = jnp.maximum(run_max, jnp.max(scores, -1))
    weights = jnp.where(valid, jnp.exp(scores - new_max[..., None]), 0.0)
    new_sum = jnp.sum(weights, -1)
    update = jnp.einsum(
        "ghrk,gkhd->grhd",
        weights.astype(jnp.bfloat16),
        value_heads,
        preferred_element_type=jnp.float32,
    )
    accum = update
    run_max, run_sum, accum = (new_max, new_sum, accum)
    att_heads = accum / jnp.transpose(run_sum, (0, 2, 1))[..., None]
    log_total = run_max + jnp.log(run_sum)
    att = att_heads.reshape(group_count, row_count, width).astype(jnp.bfloat16)
    mid = inputs + project(att, w_out)
    normed_two, inv_two = normalize(mid)
    ffn_in = (normed_two * (1.0 + scale_two[:, None, :]) + shift_two[:, None, :]).astype(
        jnp.bfloat16
    )
    upper = project(ffn_in, w_up)
    act = gelu_exact(upper).astype(jnp.bfloat16)
    out_frames = (mid + project(act, w_down)).astype(jnp.bfloat16)
    grad_out = cotangent.astype(jnp.float32)
    grad_w_down = outer_sum(act, cotangent)
    grad_upper = (back_project(cotangent, w_down) * gelu_slope(upper)).astype(jnp.bfloat16)
    grad_w_up = outer_sum(ffn_in, grad_upper)
    grad_ffn_in = back_project(grad_upper, w_up)
    grad_scale_two = jnp.sum(grad_ffn_in * normed_two, 1)
    grad_shift_two = jnp.sum(grad_ffn_in, 1)
    grad_mid = grad_out + norm_back(
        grad_ffn_in * (1.0 + scale_two[:, None, :]), normed_two, inv_two
    )
    grad_mid_low = grad_mid.astype(jnp.bfloat16)
    grad_w_out = outer_sum(att, grad_mid_low)
    grad_att = back_project(grad_mid_low, w_out).astype(jnp.bfloat16)
    grad_att_heads = grad_att.reshape(group_count, row_count, head_count, head_size)
    delta = jnp.transpose(jnp.sum(grad_att_heads.astype(jnp.float32) * att_heads, -1), (0, 2, 1))
    key_piece = lax.all_gather(key_local, "seq", axis=1, tiled=True)
    value_piece = lax.all_gather(value_local, "seq", axis=1, tiled=True)
    count = key_piece.shape[1]
    key_heads = key_piece.reshape(group_count, count, head_count, head_size)
    value_heads = value_piece.reshape(group_count, count, head_count, head_size)
    valid = key_mask(count)
    scores = (
        jnp.einsum("grhd,gkhd->ghrk", query_heads, key_heads, preferred_element_type=jnp.float32)
        * scale
    )
    probs = jnp.where(valid, jnp.exp(scores - log_total[..., None]), 0.0)
    value_part = jnp.einsum(
        "ghrk,grhd->gkhd",
        probs.astype(jnp.bfloat16),
        grad_att_heads,
        preferred_element_type=jnp.float32,
    )
    grad_probs = jnp.einsum(
        "grhd,gkhd->ghrk", grad_att_heads, value_heads, preferred_element_type=jnp.float32
    )
    grad_scores = (probs * (grad_probs - delta[..., None])).astype(jnp.bfloat16)
    grad_query = (
        jnp.einsum("ghrk,gkhd->grhd", grad_scores, key_heads, preferred_element_type=jnp.float32)
        * scale
    )
    key_part = (
        jnp.einsum("ghrk,grhd->gkhd", grad_scores, query_heads, preferred_element_type=jnp.float32)
        * scale
    )
    grad_keys = key_part.reshape(group_count, count, width)
    grad_values = value_part.reshape(group_count, count, width)
    back_result = (grad_query, grad_keys, grad_values)
    grad_query, grad_keys, grad_values = back_result
    own_keys, own_values = (
        lax.psum_scatter(
            grad_keys.astype(jnp.bfloat16), "seq", scatter_dimension=1, tiled=True
        ).astype(jnp.float32),
        lax.psum_scatter(
            grad_values.astype(jnp.bfloat16), "seq", scatter_dimension=1, tiled=True
        ).astype(jnp.float32),
    )
    grad_qkv = jnp.concatenate(
        [
            grad_query.reshape(group_count, row_count, width).astype(jnp.bfloat16),
            own_keys.astype(jnp.bfloat16),
            own_values.astype(jnp.bfloat16),
        ],
        -1,
    )
    grad_w_qkv = outer_sum(attn_in, grad_qkv)
    grad_attn_in = back_project(grad_qkv, w_qkv)
    grad_scale_one = jnp.sum(grad_attn_in * normed_one, 1)
    grad_shift_one = jnp.sum(grad_attn_in, 1)
    frames_grad = (
        grad_mid + norm_back(grad_attn_in * (1.0 + scale_one[:, None, :]), normed_one, inv_one)
    ).astype(jnp.bfloat16)
    grad_modul = jnp.concatenate(
        [grad_scale_one, grad_shift_one, grad_scale_two, grad_shift_two], -1
    )
    grad_ada = lax.dot_general(cond, grad_modul, (((0,), (0,)), ((), ())), precision=HIGHEST)
    grad_bias = jnp.sum(grad_modul, 0)
    grad_cond = lax.dot_general(grad_modul, ada_full, (((1,), (1,)), ((), ())), precision=HIGHEST)
    grad_embed = lax.dot_general(onehot, grad_cond, (((0,), (0,)), ((), ())), precision=HIGHEST)
    parts = (
        lax.psum_scatter(
            grad_embed.astype(jnp.bfloat16), "items", scatter_dimension=1, tiled=True
        ).astype(jnp.float32),
        lax.psum_scatter(
            grad_ada.astype(jnp.bfloat16), "items", scatter_dimension=0, tiled=True
        ).astype(jnp.float32),
        lax.psum_scatter(
            grad_bias.astype(jnp.bfloat16), "items", scatter_dimension=0, tiled=True
        ).astype(jnp.float32),
        lax.psum_scatter(
            grad_w_qkv.astype(jnp.bfloat16), "items", scatter_dimension=0, tiled=True
        ).astype(jnp.float32),
        lax.psum_scatter(
            grad_w_out.astype(jnp.bfloat16), "items", scatter_dimension=0, tiled=True
        ).astype(jnp.float32),
        lax.psum_scatter(
            grad_w_up.astype(jnp.bfloat16), "items", scatter_dimension=0, tiled=True
        ).astype(jnp.float32),
        lax.psum_scatter(
            grad_w_down.astype(jnp.bfloat16), "items", scatter_dimension=0, tiled=True
        ).astype(jnp.float32),
    )
    sum_embed, sum_ada, sum_bias, sum_qkv, sum_out, sum_up, sum_down = (
        lax.psum(parts[0].astype(jnp.bfloat16), "seq").astype(jnp.float32),
        lax.psum(parts[1].astype(jnp.bfloat16), "seq").astype(jnp.float32),
        lax.psum(parts[2].astype(jnp.bfloat16), "seq").astype(jnp.float32),
        lax.psum(parts[3].astype(jnp.bfloat16), "seq").astype(jnp.float32),
        lax.psum(parts[4].astype(jnp.bfloat16), "seq").astype(jnp.float32),
        lax.psum(parts[5].astype(jnp.bfloat16), "seq").astype(jnp.float32),
        lax.psum(parts[6].astype(jnp.bfloat16), "seq").astype(jnp.float32),
    )
    return (
        out_frames,
        frames_grad,
        sum_embed,
        sum_ada,
        sum_bias,
        sum_qkv,
        sum_out,
        sum_up,
        sum_down,
    )


def solution(mesh):
    in_specs = (
        P("items", "seq", None),
        P("items", "seq", None),
        P("items"),
        P("items"),
        P(),
        P(),
        P(),
        P(),
        P(),
        P(),
        P(),
    )
    out_specs = (
        P("items", "seq", None),
        P("items", "seq", None),
        P(None, "items"),
        P("items", None),
        P("items"),
        P("items", None),
        P("items", None),
        P("items", None),
        P("items", None),
    )
    return jax.shard_map(
        per_device, mesh=mesh, in_specs=in_specs, out_specs=out_specs, check_vma=False
    )
```

profile of v0, /device:TPU:0, one launch (start us, length us, event | category | flops | bytes accessed | tf_op | source)
XLA Modules:
  0.0 937.2 jit_solution(6268356600912304803)
XLA Ops:
  8.0 1.6 convert_reduce_fusion
  9.6 1.9 fusion.33
  11.8 5.8 fusion.53
  17.7 4.8 fusion.15
  22.6 2.1 fusion.74
  24.7 0.7 all-gather.3.cloned.1.call-update
  26.6 1.7 copy.35
  28.3 38.2 %all-gather.5.cloned.1.call-done = bf16[1,1280,1024]{2,1,0:T(8,128)(2,1)} async-done(((bf16[1,640,1024]{2,1,0:T(8,128)(2,1)}), bf16[1,1280,1024]{2,1,0:T(8,128)(2,1)}) %all-gather.5.cloned.1.call-update) | async-done | bytes 2621456 | tf_op jit(solution)/shard_map/all_gather | solution.py:102
  66.6 4.5 copy.36
  71.0 20.5 %select_reduce_fusion = (f32[16,640]{1,0:T(8,128)S(1)}, f32[16,640,1280]{2,1,0:T(8,128)}) fusion(pred[1280]{0:T(1024)(128)(4,1)S(1)} %fusion.52, bf16[640,16,64]{0,2,1:T(8,128)(2,1)S(1)} %bitcast.164, bf16[1280,16,64]{0,2,1:T(8,128)(2,1)} %bitcast.160), kind=kOutput, calls=%fused_computation.3 | convolution fusion | flops 1717032960 | bytes 56403200 | tf_op jit(solution)/shard_map/grhd,gkhd->ghrk/dot_general | solution.py:109
  91.5 17.1 %fusion.1 = f32[16,640]{1,0:T(8,128)S(1)} fusion(f32[16,640,1280]{2,1,0:T(8,128)} %get-tuple-element.32, f32[16,640]{1,0:T(8,128)S(1)} %broadcast_maximum_fusion, pred[1280]{0:T(1024)(128)(4,1)S(1)} %fusion.52), kind=kLoop, calls=%fused_computation.5 | loop fusion | flops 65525760 | bytes 52512000 | tf_op jit(solution)/shard_map/reduce_sum | solution.py:115
  108.6 4.4 copy.34
  113.0 22.3 %fusion.75 = (bf16[1,640,16,64]{1,3,2,0:T(8,128)(2,1)S(1)}, f32[1,640,16,64]{1,3,2,0:T(8,128)}) fusion(f32[640,16]{0,1:T(8,128)S(1)} %bitcast.178, bf16[1280,16,64]{0,2,1:T(8,128)(2,1)} %bitcast.170, f32[16,640,1280]{2,1,0:T(8,128)} %get-tuple-element.32, f32[16,640]{1,0:T(8,128)S(1)} %broadcast_maximum_fusion, pred[1280]{0:T(1024)(128)(4,1)S(1)} %fusion.52), kind=kOutput, calls=%fused_computation.117 | convolution fusion | flops 1744568320 | bytes 59065600 | tf_op jit(solution)/shard_map/ghrk,gkhd->grhd/dot_general | solution.py:116
  135.3 1.7 fusion.76
  137.4 12.4 %multiply_convert_fusion.2 = (bf16[640,4096]{1,0:T(8,128)(2,1)}, f32[640,4096]{1,0:T(8,128)}) fusion(bf16[1024,4096]{1,0:T(8,128)(2,1)} %param.20, f32[1,640,1024]{2,1,0:T(8,128)S(1)} %get-tuple-element.36, f32[1024]{0:T(1024)S(1)} %bitcast.207, f32[1024]{0:T(1024)S(1)} %bitcast.192, f32[640]{0:T(1024)S(1)} %add_rsqrt_fusion, ...), kind=kOutput, calls=%fused_computation.19 | convolution fusion | flops 5385093120 | bytes 26752000 | tf_op jit(solution)/shard_map/dot_general | solution.py:40
  149.8 14.0 %fusion.14 = bf16[640,4096]{1,0:T(8,128)(2,1)} fusion(f32[640,4096]{1,0:T(8,128)} %get-tuple-element.38, bf16[4096,1024]{1,0:T(8,128)(2,1)} %param.21, bf16[1,640,1024]{2,1,0:T(8,128)(2,1)S(1)} %copy-done.13), kind=kOutput, calls=%fused_computation.18 | convolution fusion | flops 5394923520 | bytes 25427968 | tf_op jit(solution)/shard_map/dot_general | solution.py:46
  163.8 8.4 fusion.34
  172.6 1.0 fusion.37
  173.7 1.5 copy-done.8
  175.2 1.6 convolution_convert_fusion.5
  176.8 0.7 copy.37
  177.5 1.9 copy.38
  179.4 21.4 %fusion.16 = bf16[16,64,1280]{2,1,0:T(8,128)(2,1)} fusion(bf16[640,16,64]{0,2,1:T(8,128)(2,1)S(1)} %bitcast.175, f32[16,640,1280]{2,1,0:T(8,128)} %get-tuple-element.32, f32[16,640]{1,0:T(8,128)S(1)} %log_add_fusion, pred[1280]{0:T(1024)(128)(4,1)S(1)} %fusion.52), kind=kOutput, calls=%fused_computation.31 | convolution fusion | flops 1731461120 | bytes 56403200 | tf_op jit(solution)/shard_map/ghrk,grhd->gkhd/dot_general | solution.py:161
  200.8 11.5 %copy.41 = bf16[1,1280,1024]{2,0,1:T(2,128)(2,1)} copy(bf16[1,1280,1024]{1,2,0:T(8,128)(2,1)} %bitcast.172) | data formatting | bytes 5242880
  212.4 5.0 copy.49
  217.5 3.1 multiply_reduce_fusion
  221.2 33.9 %multiply_convert_fusion = bf16[16,640,1280]{2,1,0:T(8,128)(2,1)} fusion(f32[16,640,1280]{2,1,0:T(8,128)} %get-tuple-element.32, bf16[640,16,64]{0,2,1:T(8,128)(2,1)S(1)} %bitcast.176, bf16[1280,16,64]{0,2,1:T(8,128)(2,1)S(1)} %bitcast.171, f32[16,640]{1,0:T(8,128)S(1)} %bitcast.184, f32[16,640]{1,0:T(8,128)S(1)} %log_add_fusion, pred[1280]{0:T(1024)(128)(4,1)S(1)} %fusion.52), kind=kOutput, calls=%fused_computation | convolution fusion | flops 1756364800 | bytes 82658560 | tf_op jit(solution)/shard_map/grhd,gkhd->ghrk/dot_general | solution.py:167
  255.0 14.6 %multiply_convert_fusion.3 = bf16[16,64,1280]{2,1,0:T(8,128)(2,1)} fusion(bf16[640,16,64]{0,2,1:T(8,128)(2,1)S(1)} %bitcast.165, bf16[16,640,1280]{2,1,0:T(8,128)(2,1)} %multiply_convert_fusion), kind=kOutput, calls=%fused_computation.24 | convolution fusion | flops 1680343040 | bytes 30146560 | tf_op jit(solution)/shard_map/ghrk,grhd->gkhd/dot_general | solution.py:176
  269.6 11.6 %copy.39 = bf16[1,1280,1024]{2,0,1:T(2,128)(2,1)} copy(bf16[1,1280,1024]{1,2,0:T(8,128)(2,1)} %bitcast.166) | data formatting | bytes 5242880
  281.2 5.0 copy.50
  286.7 0.8 copy-done.30
  287.6 4.8 convolution_convert_fusion.4
  292.5 12.2 %convolution_convert_fusion = bf16[1024,4096]{1,0:T(8,128)(2,1)} fusion(bf16[640,4096]{1,0:T(8,128)(2,1)} %fusion.14, f32[1,640,1024]{2,1,0:T(8,128)} %copy-done.9, f32[1024]{0:T(1024)S(1)} %bitcast.208, f32[1024]{0:T(1024)S(1)} %bitcast.196, f32[640]{0:T(1024)S(1)} %add_rsqrt_fusion, f32[640]{0:T(1024)S(1)} %broadcast_multiply_fusion.4), kind=kOutput, calls=%fused_computation.21 | convolution fusion | flops 5376180224 | bytes 16266240 | tf_op jit(solution)/shard_map/dot_general | solution.py:55
  304.8 1.2 copy-done.14
  306.0 11.5 %convolution_convert_fusion.1 = bf16[4096,1024]{1,0:T(8,128)(2,1)} fusion(bf16[640,4096]{1,0:T(8,128)(2,1)} %get-tuple-element.37, bf16[1,640,1024]{2,1,0:T(8,128)(2,1)S(1)} %copy-done.14), kind=kOutput, calls=%fused_computation.22 | convolution fusion | flops 5372903424 | bytes 14942208 | tf_op jit(solution)/shard_map/dot_general | solution.py:55
  317.7 13.9 %multiply_convert_fusion.4 = bf16[16,64,640]{2,1,0:T(8,128)(2,1)S(1)} fusion(bf16[1280,16,64]{0,2,1:T(8,128)(2,1)} %bitcast.161, bf16[16,640,1280]{2,1,0:T(8,128)(2,1)} %multiply_convert_fusion), kind=kOutput, calls=%fused_computation.61 | convolution fusion | flops 1679032320 | bytes 30146560 | tf_op jit(solution)/shard_map/ghrk,gkhd->grhd/dot_general | solution.py:172
  331.7 4.2 reshape_bitcast_fusion
  335.9 6.1 copy.42
  342.0 4.2 reshape_bitcast_fusion.1
  346.3 6.2 copy.40
  352.5 9.9 %convolution_convert_fusion.2 = bf16[1024,3072]{1,0:T(8,128)(2,1)} fusion(bf16[1,640,1024]{1,2,0:T(8,128)(2,1)} %copy.42, bf16[1,640,1024]{1,2,0:T(8,128)(2,1)} %copy.40, bf16[1,640,1024]{1,2,0:T(8,128)(2,1)S(1)} %bitcast.173, bf16[1,640,1024]{2,1,0:T(8,128)(2,1)S(1)} %copy-done.6, f32[1024]{0:T(1024)S(1)} %bitcast.206, f32[1024]{0:T(1024)S(1)} %bitcast.186, ...), kind=kOutput, calls=%fused_computation.23 | convolution fusion | flops 4045406208 | bytes 11547648 | tf_op jit(solution)/shard_map/dot_general | solution.py:55
  362.7 8.7 fusion.32
  371.4 1.5 copy-done.7
  373.3 5.2 multiply_convert_fusion.1
  378.6 8.9 fusion.50
  387.6 0.9 copy.43
  388.5 0.6 dynamic-slice
  389.8 106.1 %reduce-scatter.21.cloned.1.call-done = bf16[64,4096]{1,0:T(8,128)(2,1)} async-done(((bf16[1024,4096]{1,0:T(8,128)(2,1)}), bf16[64,4096]{1,0:T(8,128)(2,1)}) %reduce-scatter.21.cloned.1.call-update) | async-done | bytes 524304 | tf_op jit(solution)/shard_map/reduce_scatter | solution.py:229
  495.9 107.2 %reduce-scatter.23.cloned.1.call-done = bf16[256,1024]{1,0:T(8,128)(2,1)} async-done(((bf16[4096,1024]{1,0:T(8,128)(2,1)}), bf16[256,1024]{1,0:T(8,128)(2,1)}) %reduce-scatter.23.cloned.1.call-update) | async-done | bytes 524304 | tf_op jit(solution)/shard_map/reduce_scatter | solution.py:232
  603.1 88.6 %reduce-scatter.17.cloned.1.call-done = bf16[64,3072]{1,0:T(8,128)(2,1)} async-done(((bf16[1024,3072]{1,0:T(8,128)(2,1)}), bf16[64,3072]{1,0:T(8,128)(2,1)}) %reduce-scatter.17.cloned.1.call-update) | async-done | bytes 393232 | tf_op jit(solution)/shard_map/reduce_scatter | solution.py:223
  691.7 106.7 %reduce-scatter.15.cloned.1.call-done = bf16[64,4096]{1,0:T(8,128)(2,1)} async-done(((bf16[1024,4096]{1,0:T(8,128)(2,1)}), bf16[64,4096]{1,0:T(8,128)(2,1)}) %reduce-scatter.15.cloned.1.call-update) | async-done | bytes 524304 | tf_op jit(solution)/shard_map/reduce_scatter | solution.py:217
  798.4 10.8 %fusion.38 = bf16[1,640,1024]{2,1,0:T(8,128)(2,1)} fusion(f32[1,640,1024]{2,1,0:T(8,128)} %copy-done.9, bf16[640,4096]{1,0:T(8,128)(2,1)} %get-tuple-element.37, bf16[4096,1024]{1,0:T(8,128)(2,1)} %param.21), kind=kOutput, calls=%fused_computation.60 | convolution fusion | flops 5370019840 | bytes 17563648 | tf_op jit(solution)/shard_map/dot_general | solution.py:40
  809.2 32.7 %all-reduce = bf16[4096]{0:T(1024)(128)(2,1)S(1)} all-reduce(bf16[4096]{0:T(1024)(128)(2,1)S(1)} %convert_element_type.227), channel_id=6, replica_groups=mesh['items'=16,'seq'=2] {'items'}, use_global_device_ids=true, to_apply=%region_21.22.clone | all-reduce | flops 4096 | bytes 16384
  842.0 3.9 fusion.31
  845.9 11.9 %reduce-scatter.29.cloned.1.call-done = bf16[64,8]{1,0:T(8,128)(2,1)} async-done(((bf16[1024,8]{1,0:T(8,128)(2,1)}), bf16[64,8]{1,0:T(8,128)(2,1)}) %reduce-scatter.29.cloned.1.call-update) | async-done | bytes 1040
  857.8 0.8 copy.44
  858.6 4.9 all-reduce.1
  864.0 0.6 convert_element_type.224
  864.6 57.8 %all-reduce.5.cloned.1.call-done = (bf16[64,4096]{1,0:T(8,128)(2,1)}, bf16[64,3072]{1,0:T(8,128)(2,1)}, bf16[64,1024]{1,0:T(8,128)(2,1)}, bf16[64,4096]{1,0:T(8,128)(2,1)}, bf16[256,1024]{1,0:T(8,128)(2,1)}) async-done(((bf16[64,4096]{1,0:T(8,128)(2,1)}, bf16[64,3072]{1,0:T(8,128)(2,1)}, bf16[64,1024]{1,0:T(8,128)(2,1)}, bf16[64,4096]{1,0:T(8,128)(2,1)}, bf16[256,1024]{1,0:T(8,128)(2,1)}), ...) | async-done | bytes 2097168 | tf_op jit(solution)/shard_map/psum | solution.py:238
  922.4 1.7 convert_element_type.232
  924.1 2.2 convert_element_type.226
  926.4 1.9 convert_element_type.230
  928.3 1.0 convert_element_type.234
  929.3 1.1 convert_element_type.236
  (117 shorter events, 4.7 us)
Async XLA Ops:
  7.2 128.1 %copy-start = (bf16[1024,1024]{1,0:T(8,128)(2,1)S(1)}, bf16[1024,1024]{1,0:T(8,128)(2,1)}, u32[]{:S(2)}) copy-start(bf16[1024,1024]{1,0:T(8,128)(2,1)} %param.19) | copy-start | bytes 6291460
  7.2 4.4 copy-start.23
  7.2 59.4 %all-gather.5.cloned.1.call-start = ((), (), s32[]{:S(2)}) async-start(), calls=%async_computation.9 | async-start | bytes 3932160 | tf_op jit(solution)/shard_map/all_gather | solution.py:102
  9.6 8.1 copy-start.19
  9.6 8.1 slice-start.2
  11.6 6.1 copy-start.24
  11.7 5.9 copy-start.17
  11.8 5.9 copy-start.26
  11.8 5.9 copy-start.4
  11.8 5.9 slice-start.3
  17.7 4.9 copy-start.21
  17.7 4.9 copy-start.27
  24.7 83.9 %all-gather.3.cloned.1.call-start = ((), (), s32[]{:S(2)}) async-start(), calls=%async_computation.8 | async-start | bytes 3932160 | tf_op jit(solution)/shard_map/all_gather | solution.py:103
  25.4 306.2 %reduce-scatter.27.cloned.1.call-start = ((), (), s32[]{:S(2)}) async-start(), calls=%async_computation.16 | async-start | bytes 3932160
  28.3 42.7 %copy-start.2 = (bf16[1,640,1024]{1,2,0:T(8,128)(2,1)}, bf16[1,640,1024]{1,2,0:T(8,128)(2,1)S(1)}, u32[]{:S(2)}) copy-start(bf16[1,640,1024]{1,2,0:T(8,128)(2,1)S(1)} %copy.35) | copy-start | bytes 3932164
  113.0 22.3 %copy-start.5 = (bf16[1,640,1024]{2,1,0:T(8,128)(2,1)S(1)}, bf16[1,640,1024]{2,1,0:T(8,128)(2,1)}, u32[]{:S(2)}) copy-start(bf16[1,640,1024]{2,1,0:T(8,128)(2,1)} %param.11) | copy-start | bytes 3932164
  135.3 1.7 copy-start.29
  137.0 35.6 %copy-start.9 = (f32[1,640,1024]{2,1,0:T(8,128)}, f32[1,640,1024]{2,1,0:T(8,128)S(1)}, u32[]{:S(2)}) copy-start(f32[1,640,1024]{2,1,0:T(8,128)S(1)} %get-tuple-element.36) | copy-start | bytes 7864324
  137.4 12.4 %copy-start.13 = (bf16[1,640,1024]{2,1,0:T(8,128)(2,1)S(1)}, bf16[1,640,1024]{2,1,0:T(8,128)(2,1)}, u32[]{:S(2)}) copy-start(bf16[1,640,1024]{2,1,0:T(8,128)(2,1)} %param.12) | copy-start | bytes 3932164
  137.4 26.4 %slice-start = ((s8[8388608]{0:T(1024)(128)(4,1)}), s8[4194304]{0:T(1024)(128)(4,1)S(1)}, s32[]{:S(2)}) async-start(s8[8388608]{0:T(1024)(128)(4,1)} %bitcast.209), calls=%async_computation.19 | async-start | bytes 8388608
  149.8 14.0 %slice-start.1 = ((s8[8388608]{0:T(1024)(128)(4,1)}), s8[4194304]{0:T(1024)(128)(4,1)S(1)}, s32[]{:S(2)}) async-start(s8[8388608]{0:T(1024)(128)(4,1)} %bitcast.209), calls=%async_computation.20 | async-start | bytes 8388608
  173.7 1.5 copy-start.8
  177.5 23.3 %copy-start.11 = (bf16[640,1024]{0,1:T(8,128)(2,1)}, bf16[640,1024]{0,1:T(8,128)(2,1)S(1)}, u32[]{:S(2)}) copy-start(bf16[640,1024]{0,1:T(8,128)(2,1)S(1)} %copy.37) | copy-start | bytes 3932164
  217.4 124.6 %reduce-scatter.25.cloned.1.call-start = ((), (), s32[]{:S(2)}) async-start(), calls=%async_computation.15 | async-start | bytes 3932160
  217.5 3.3 copy-start.10
  217.5 3.7 copy-start.12
  221.2 33.9 %copy-start.3 = (bf16[1,640,1024]{1,2,0:T(8,128)(2,1)S(1)}, bf16[1,640,1024]{1,2,0:T(8,128)(2,1)}, u32[]{:S(2)}) copy-start(bf16[1,640,1024]{1,2,0:T(8,128)(2,1)} %copy-done.2) | copy-start | bytes 3932164
  286.2 1.3 copy-start.30
  286.3 103.5 %reduce-scatter.19.cloned.1.call-start = ((), (), s32[]{:S(2)}) async-start(), calls=%async_computation.12 | async-start | bytes 2228224 | tf_op jit(solution)/shard_map/reduce_scatter | solution.py:226
  292.4 203.5 %reduce-scatter.21.cloned.1.call-start = ((), (), s32[]{:S(2)}) async-start(), calls=%async_computation.13 | async-start | bytes 8912896 | tf_op jit(solution)/shard_map/reduce_scatter | solution.py:229
  304.7 1.3 copy-start.14
  304.7 298.4 %reduce-scatter.23.cloned.1.call-start = ((), (), s32[]{:S(2)}) async-start(), calls=%async_computation.14 | async-start | bytes 8912896 | tf_op jit(solution)/shard_map/reduce_scatter | solution.py:232
  317.5 374.2 %reduce-scatter.17.cloned.1.call-start = ((), (), s32[]{:S(2)}) async-start(), calls=%async_computation.11 | async-start | bytes 6684672 | tf_op jit(solution)/shard_map/reduce_scatter | solution.py:223
  346.3 6.2 copy-start.6
  346.3 6.2 copy-start.20
  346.3 6.2 copy-start.22
  346.3 6.3 copy-start.25
  346.3 6.3 copy-start.28
  362.4 436.0 %reduce-scatter.15.cloned.1.call-start = ((), (), s32[]{:S(2)}) async-start(), calls=%async_computation.10 | async-start | bytes 8912896 | tf_op jit(solution)/shard_map/reduce_scatter | solution.py:217
  371.4 1.5 copy-start.7
  371.4 1.9 copy-start.18
  378.5 479.3 %reduce-scatter.29.cloned.1.call-start = ((), (), s32[]{:S(2)}) async-start(), calls=%async_computation.17 | async-start | bytes 278528
  378.6 9.9 %copy-start.31 = (u32[32]{0:T(128)S(1)}, u32[32]{0:T(128)}, u32[]{:S(2)}) copy-start(u32[32]{0:T(128)} %constant.42) | copy-start | bytes 388
  388.4 534.0 %all-reduce.5.cloned.1.call-start = ((), (), s32[]{:S(2)}) async-start(), calls=%async_computation.18 | async-start | bytes 4194304 | tf_op jit(solution)/shard_map/psum | solution.py:238
  922.4 5.9 copy-start.16
  922.4 6.9 copy-start.15
  924.1 6.3 copy-start.1
Sparse Core Ops, SparseCore 0:
  24.8 41.7 all-gather.4
  68.1 38.9 all-gather.2
  217.6 37.9 reduce-scatter.26
  286.4 37.7 reduce-scatter.24
  327.8 61.7 reduce-scatter.18
  393.5 102.3 reduce-scatter.20
  500.0 103.0 reduce-scatter.22
  607.0 84.6 reduce-scatter.16
  695.8 102.5 reduce-scatter.14
  802.4 55.3 reduce-scatter.28
  860.3 62.0 all-reduce.4
where the time goes:
time: 943 us; the launch traced here: 937 us
  waiting for transfers between devices  517 us (55%)
  matrix products  242 us (26%)
  local copies, waits for them, and re-layouts  77.4 us (8%)
  other arithmetic  44.1 us (5%)
  blocking collectives  37.6 us (4%)
  between operations  16.7 us (2%)
    reduce_scatter x1, waiting for transfers between devices, per_device(): lax.psum_scatter(grad_w_down.astype(jnp.bfloat16), 'items', scatter_dimen...  107 us
    reduce_scatter x1, waiting for transfers between devices, per_device(): lax.psum_scatter(grad_ada.astype(jnp.bfloat16), 'items', scatter_dimensio...  107 us
    reduce_scatter x1, waiting for transfers between devices, per_device(): lax.psum_scatter(grad_w_up.astype(jnp.bfloat16), 'items', scatter_dimensi...  106 us
    reduce_scatter x1, waiting for transfers between devices, per_device(): lax.psum_scatter(grad_w_qkv.astype(jnp.bfloat16), 'items', scatter_dimens...  88.6 us
    unnamed x84, local copies, waits for them, and re-layouts  62.1 us
    psum x1, waiting for transfers between devices, per_device(): lax.psum(parts[1].astype(jnp.bfloat16), 'seq').astype(jnp.float32)  57.8 us
    dot_general x4, matrix products, outer_sum(): lax.dot_general(left_flat, right_flat, (((0,), (0,)), ((), ())), preferre...  38.4 us
    all_gather x1, waiting for transfers between devices, per_device(): key_piece = lax.all_gather(key_local, 'seq', axis=1, tiled=True)  38.2 us
  transfers between devices with their start and end apart: 11, of which 7 were waited for; matrix products, arithmetic and copies ran while one was open for 24% of the time, Pallas kernels for 0%

commit v1 on v0

--- a/solution.py
+++ b/solution.py
@@ -99,8 +99,13 @@
         return valid[:, None, None, :]
 
     run_max = jnp.full((group_count, head_count, row_count), NEGATIVE, jnp.float32)
-    key_piece = lax.all_gather(key_local, "seq", axis=1, tiled=True)
-    value_piece = lax.all_gather(value_local, "seq", axis=1, tiled=True)
+    key_piece, value_piece = jnp.split(
+        lax.all_gather(
+            jnp.concatenate([key_local, value_local], axis=0), "seq", axis=1, tiled=True
+        ),
+        [key_local.shape[0]],
+        axis=0,
+    )
     count = key_piece.shape[1]
     key_heads = key_piece.reshape(group_count, count, head_count, head_size)
     value_heads = value_piece.reshape(group_count, count, head_count, head_size)

time: 943 us -> 1070 us (1.13)
  waiting for transfers between devices: 517 us -> 593 us
  matrix products: 242 us -> 276 us
  local copies, waits for them, and re-layouts: 77.4 us -> 93 us
    all_gather x0 -> x1, waiting for transfers between devices: none -> 42.6 us  [per_device(): lax.all_gather(jnp.concatenate([key_local, value_local], axis=0), 'seq',...]
    all_gather x1, waiting for transfers between devices: 0.02 us -> 34.7 us  [per_device(): value_piece = lax.all_gather(value_local, 'seq', axis=1, tiled=True)]
    dot_general x1 -> x2, matrix products: 20.5 us -> 43.2 us  [per_device(): jnp.einsum('grhd,gkhd->ghrk', query_heads, key_heads, preferred_element_t...]
    split x0 -> x3, local copies, waits for them, and re-layouts: none -> 14.3 us  [per_device(): jnp.split(lax.all_gather(jnp.concatenate([key_local, value_local], axis=0...]
    dot_general x4, matrix products: 29.6 us -> 42 us  [project(): result = jnp.dot(flat, weight, preferred_element_type=jnp.float32)]
    unnamed x84 -> x88, local copies, waits for them, and re-layouts: 62.1 us -> 63.1 us
  transfers between devices with their start and end apart: 11 -> 12, of which waited for: 7 -> 9; matrix products, arithmetic and copies ran while one was open for 24% -> 21% of each run, Pallas kernels for 0% -> 0%
where the time goes in v1:
time: 1070 us; the launch traced here: 1060 us
  waiting for transfers between devices  593 us (55%)
  matrix products  276 us (26%)
  local copies, waits for them, and re-layouts  93 us (9%)
  other arithmetic  47.3 us (4%)
  blocking collectives  37.5 us (4%)
  between operations  17.1 us (2%)
    reduce_scatter x1, waiting for transfers between devices, per_device(): lax.psum_scatter(grad_w_down.astype(jnp.bfloat16), 'items', scatter_dimen...  107 us
    reduce_scatter x1, waiting for transfers between devices, per_device(): lax.psum_scatter(grad_ada.astype(jnp.bfloat16), 'items', scatter_dimensio...  107 us
    reduce_scatter x1, waiting for transfers between devices, per_device(): lax.psum_scatter(grad_w_up.astype(jnp.bfloat16), 'items', scatter_dimensi...  106 us
    reduce_scatter x1, waiting for transfers between devices, per_device(): lax.psum_scatter(grad_w_qkv.astype(jnp.bfloat16), 'items', scatter_dimens...  88.7 us
    unnamed x88, local copies, waits for them, and re-layouts  63.1 us
    psum x1, waiting for transfers between devices, per_device(): lax.psum(parts[1].astype(jnp.bfloat16), 'seq').astype(jnp.float32)  57.7 us
    dot_general x2, matrix products, per_device(): jnp.einsum('grhd,gkhd->ghrk', query_heads, key_heads, preferred_element_t...  43.2 us
    all_gather x1, waiting for transfers between devices, per_device(): lax.all_gather(jnp.concatenate([key_local, value_local], axis=0), 'seq',...  42.6 us
  transfers between devices with their start and end apart: 12, of which 9 were waited for; matrix products, arithmetic and copies ran while one was open for 21% of the time, Pallas kernels for 0%

profile of v1, /device:TPU:0, one launch (start us, length us, event | category | flops | bytes accessed | tf_op | source)
XLA Modules:
  0.0 1063.9 jit_solution(12498574730431113425)
XLA Ops:
  8.0 1.6 convert_reduce_fusion
  9.6 1.9 fusion.34
  11.8 5.8 fusion.54
  17.7 4.8 fusion.16
  22.6 2.0 fusion.76
  25.9 3.1 pad_maximum_fusion
  29.7 2.1 copy.39
  31.8 34.7 %all-gather.8.cloned.1.call-done = bf16[1,1280,1024]{2,1,0:T(8,128)(2,1)} async-done(((bf16[1,640,1024]{2,1,0:T(8,128)(2,1)}), bf16[1,1280,1024]{2,1,0:T(8,128)(2,1)}) %all-gather.8.cloned.1.call-update) | async-done | bytes 2621456 | tf_op jit(solution)/shard_map/all_gather | solution.py:156
  66.5 4.4 copy.43
  70.9 36.2 %all-gather.6.cloned.1.call-done = bf16[1,1280,1024]{2,1,0:T(8,128)(2,1)} async-done(((bf16[1,640,1024]{2,1,0:T(8,128)(2,1)}), bf16[1,1280,1024]{2,1,0:T(8,128)(2,1)}) %all-gather.6.cloned.1.call-update) | async-done | bytes 2621456 | tf_op jit(solution)/shard_map/all_gather | solution.py:155
  107.1 4.4 copy.41
  111.5 23.2 %fusion.79 = f32[16,640,1280]{2,1,0:T(8,128)} fusion(bf16[640,16,64]{0,2,1:T(8,128)(2,1)S(1)} %bitcast.166, bf16[1280,16,64]{0,2,1:T(8,128)(2,1)} %bitcast.164), kind=kOutput, calls=%fused_computation.122 | convolution fusion | flops 1677721600 | bytes 56360960 | tf_op jit(solution)/shard_map/grhd,gkhd->ghrk/dot_general | solution.py:162
  134.6 42.6 %all-gather.4.cloned.1.call-done = bf16[2,1280,1024]{2,1,0:T(8,128)(2,1)} async-done(((bf16[2,640,1024]{2,1,0:T(8,128)(2,1)}), bf16[2,1280,1024]{2,1,0:T(8,128)(2,1)}) %all-gather.4.cloned.1.call-update) | async-done | bytes 5242896 | tf_op jit(solution)/shard_map/all_gather | solution.py:103
  177.2 5.4 fusion.75
  182.6 4.5 copy.40
  187.0 4.4 copy.38
  191.5 20.0 %fusion = (f32[16,640]{1,0:T(8,128)S(1)}, f32[16,640,1280]{2,1,0:T(8,128)}) fusion(pred[1280]{0:T(1024)(128)(4,1)S(1)} %fusion.53, bf16[640,16,64]{0,2,1:T(8,128)(2,1)S(1)} %bitcast.167, bf16[1280,16,64]{0,2,1:T(8,128)(2,1)} %bitcast.171), kind=kOutput, calls=%fused_computation.4 | convolution fusion | flops 1717032960 | bytes 56403200 | tf_op jit(solution)/shard_map/grhd,gkhd->ghrk/dot_general | solution.py:114
  211.5 17.2 %fusion.2 = f32[16,640]{1,0:T(8,128)S(1)} fusion(f32[16,640,1280]{2,1,0:T(8,128)} %get-tuple-element.34, f32[16,640]{1,0:T(8,128)S(1)} %broadcast_maximum_fusion, pred[1280]{0:T(1024)(128)(4,1)S(1)} %fusion.53), kind=kLoop, calls=%fused_computation.6 | loop fusion | flops 65525760 | bytes 52512000 | tf_op jit(solution)/shard_map/reduce_sum | solution.py:120
  228.8 20.5 %fusion.77 = (bf16[1,640,16,64]{1,3,2,0:T(8,128)(2,1)S(1)}, f32[1,640,16,64]{1,3,2,0:T(8,128)}) fusion(f32[640,16]{0,1:T(8,128)S(1)} %bitcast.184, bf16[1280,16,64]{0,2,1:T(8,128)(2,1)S(1)} %bitcast.177, f32[16,640,1280]{2,1,0:T(8,128)} %get-tuple-element.34, f32[16,640]{1,0:T(8,128)S(1)} %broadcast_maximum_fusion, pred[1280]{0:T(1024)(128)(4,1)S(1)} %fusion.53), kind=kOutput, calls=%fused_computation.120 | convolution fusion | flops 1744568320 | bytes 59065600 | tf_op jit(solution)/shard_map/ghrk,gkhd->grhd/dot_general | solution.py:121
  249.3 1.7 fusion.78
  251.5 24.6 %multiply_convert_fusion.2 = (bf16[640,4096]{1,0:T(8,128)(2,1)}, f32[640,4096]{1,0:T(8,128)}) fusion(bf16[1024,4096]{1,0:T(8,128)(2,1)} %param.20, f32[1,640,1024]{2,1,0:T(8,128)S(1)} %get-tuple-element.38, f32[1024]{0:T(1024)S(1)} %bitcast.213, f32[1024]{0:T(1024)S(1)} %bitcast.196, f32[640]{0:T(1024)S(1)} %add_rsqrt_fusion, ...), kind=kOutput, calls=%fused_computation.20 | convolution fusion | flops 5385093120 | bytes 26752000 | tf_op jit(solution)/shard_map/dot_general | solution.py:40
  276.1 13.8 %fusion.15 = bf16[640,4096]{1,0:T(8,128)(2,1)} fusion(f32[640,4096]{1,0:T(8,128)} %get-tuple-element.40, bf16[4096,1024]{1,0:T(8,128)(2,1)} %param.21, bf16[1,640,1024]{2,1,0:T(8,128)(2,1)S(1)} %copy-done.15), kind=kOutput, calls=%fused_computation.19 | convolution fusion | flops 5394923520 | bytes 25427968 | tf_op jit(solution)/shard_map/dot_general | solution.py:46
  289.9 8.5 fusion.35
  299.7 1.5 copy-done.9
  301.3 1.6 convolution_convert_fusion.5
  303.6 1.9 copy.44
  305.5 21.4 %fusion.17 = bf16[16,64,1280]{2,1,0:T(8,128)(2,1)} fusion(bf16[640,16,64]{0,2,1:T(8,128)(2,1)S(1)} %bitcast.181, f32[16,640,1280]{2,1,0:T(8,128)} %fusion.79, f32[16,640]{1,0:T(8,128)S(1)} %log_add_fusion, pred[1280]{0:T(1024)(128)(4,1)S(1)} %fusion.53), kind=kOutput, calls=%fused_computation.32 | convolution fusion | flops 1731461120 | bytes 56403200 | tf_op jit(solution)/shard_map/ghrk,grhd->gkhd/dot_general | solution.py:166
  326.9 11.5 %copy.47 = bf16[1,1280,1024]{2,0,1:T(2,128)(2,1)} copy(bf16[1,1280,1024]{1,2,0:T(8,128)(2,1)} %bitcast.178) | data formatting | bytes 5242880
  338.4 5.1 copy.55
  343.6 3.1 multiply_reduce_fusion
  347.3 34.2 %multiply_convert_fusion = bf16[16,640,1280]{2,1,0:T(8,128)(2,1)} fusion(f32[16,640,1280]{2,1,0:T(8,128)} %fusion.79, bf16[640,16,64]{0,2,1:T(8,128)(2,1)S(1)} %bitcast.182, bf16[1280,16,64]{0,2,1:T(8,128)(2,1)S(1)} %bitcast.176, f32[16,640]{1,0:T(8,128)S(1)} %bitcast.190, f32[16,640]{1,0:T(8,128)S(1)} %log_add_fusion, pred[1280]{0:T(1024)(128)(4,1)S(1)} %fusion.53), kind=kOutput, calls=%fused_computation | convolution fusion | flops 1756364800 | bytes 82658560 | tf_op jit(solution)/shard_map/grhd,gkhd->ghrk/dot_general | solution.py:172
  381.5 14.6 %multiply_convert_fusion.3 = bf16[16,64,1280]{2,1,0:T(8,128)(2,1)} fusion(bf16[640,16,64]{0,2,1:T(8,128)(2,1)S(1)} %bitcast.168, bf16[16,640,1280]{2,1,0:T(8,128)(2,1)} %multiply_convert_fusion), kind=kOutput, calls=%fused_computation.25 | convolution fusion | flops 1680343040 | bytes 30146560 | tf_op jit(solution)/shard_map/ghrk,grhd->gkhd/dot_general | solution.py:181
  396.1 11.6 %copy.45 = bf16[1,1280,1024]{2,0,1:T(2,128)(2,1)} copy(bf16[1,1280,1024]{1,2,0:T(8,128)(2,1)} %bitcast.172) | data formatting | bytes 5242880
  407.7 5.0 copy.56
  412.7 1.2 copy-done.32
  414.0 4.8 convolution_convert_fusion.4
  418.9 12.2 %convolution_convert_fusion = bf16[1024,4096]{1,0:T(8,128)(2,1)} fusion(bf16[640,4096]{1,0:T(8,128)(2,1)} %fusion.15, f32[1,640,1024]{2,1,0:T(8,128)} %copy-done.10, f32[1024]{0:T(1024)S(1)} %bitcast.214, f32[1024]{0:T(1024)S(1)} %bitcast.200, f32[640]{0:T(1024)S(1)} %add_rsqrt_fusion, f32[640]{0:T(1024)S(1)} %broadcast_multiply_fusion.4), kind=kOutput, calls=%fused_computation.22 | convolution fusion | flops 5376180224 | bytes 16266240 | tf_op jit(solution)/shard_map/dot_general | solution.py:55
  431.2 1.2 copy-done.16
  432.4 11.5 %convolution_convert_fusion.1 = bf16[4096,1024]{1,0:T(8,128)(2,1)} fusion(bf16[640,4096]{1,0:T(8,128)(2,1)} %get-tuple-element.39, bf16[1,640,1024]{2,1,0:T(8,128)(2,1)S(1)} %copy-done.16), kind=kOutput, calls=%fused_computation.23 | convolution fusion | flops 5372903424 | bytes 14942208 | tf_op jit(solution)/shard_map/dot_general | solution.py:55
  444.0 14.1 %multiply_convert_fusion.4 = bf16[16,64,640]{2,1,0:T(8,128)(2,1)S(1)} fusion(bf16[1280,16,64]{0,2,1:T(8,128)(2,1)} %bitcast.165, bf16[16,640,1280]{2,1,0:T(8,128)(2,1)} %multiply_convert_fusion), kind=kOutput, calls=%fused_computation.63 | convolution fusion | flops 1679032320 | bytes 30146560 | tf_op jit(solution)/shard_map/ghrk,gkhd->grhd/dot_general | solution.py:177
  458.1 4.3 reshape_bitcast_fusion
  462.3 6.2 copy.48
  468.5 4.2 reshape_bitcast_fusion.1
  472.7 6.2 copy.46
  479.0 9.9 convolution_convert_fusion.2
  489.1 8.7 fusion.33
  497.8 1.5 copy-done.8
  499.7 5.2 multiply_convert_fusion.1
  505.0 8.9 fusion.51
  516.2 106.2 %reduce-scatter.21.cloned.1.call-done = bf16[64,4096]{1,0:T(8,128)(2,1)} async-done(((bf16[1024,4096]{1,0:T(8,128)(2,1)}), bf16[64,4096]{1,0:T(8,128)(2,1)}) %reduce-scatter.21.cloned.1.call-update) | async-done | bytes 524304 | tf_op jit(solution)/shard_map/reduce_scatter | solution.py:234
  622.4 107.2 %reduce-scatter.23.cloned.1.call-done = bf16[256,1024]{1,0:T(8,128)(2,1)} async-done(((bf16[4096,1024]{1,0:T(8,128)(2,1)}), bf16[256,1024]{1,0:T(8,128)(2,1)}) %reduce-scatter.23.cloned.1.call-update) | async-done | bytes 524304 | tf_op jit(solution)/shard_map/reduce_scatter | solution.py:237
  729.6 88.7 %reduce-scatter.17.cloned.1.call-done = bf16[64,3072]{1,0:T(8,128)(2,1)} async-done(((bf16[1024,3072]{1,0:T(8,128)(2,1)}), bf16[64,3072]{1,0:T(8,128)(2,1)}) %reduce-scatter.17.cloned.1.call-update) | async-done | bytes 393232 | tf_op jit(solution)/shard_map/reduce_scatter | solution.py:228
  818.2 106.5 %reduce-scatter.15.cloned.1.call-done = bf16[64,4096]{1,0:T(8,128)(2,1)} async-done(((bf16[1024,4096]{1,0:T(8,128)(2,1)}), bf16[64,4096]{1,0:T(8,128)(2,1)}) %reduce-scatter.15.cloned.1.call-update) | async-done | bytes 524304 | tf_op jit(solution)/shard_map/reduce_scatter | solution.py:222
  924.8 10.8 %fusion.39 = bf16[1,640,1024]{2,1,0:T(8,128)(2,1)} fusion(f32[1,640,1024]{2,1,0:T(8,128)} %copy-done.10, bf16[640,4096]{1,0:T(8,128)(2,1)} %get-tuple-element.39, bf16[4096,1024]{1,0:T(8,128)(2,1)} %param.21), kind=kOutput, calls=%fused_computation.62 | convolution fusion | flops 5370019840 | bytes 17563648 | tf_op jit(solution)/shard_map/dot_general | solution.py:40
  935.6 32.6 %all-reduce = bf16[4096]{0:T(1024)(128)(2,1)S(1)} all-reduce(bf16[4096]{0:T(1024)(128)(2,1)S(1)} %convert_element_type.227), channel_id=6, replica_groups=mesh['items'=16,'seq'=2] {'items'}, use_global_device_ids=true, to_apply=%region_21.22.clone | all-reduce | flops 4096 | bytes 16384
  968.3 3.9 fusion.32
  972.2 12.1 %reduce-scatter.29.cloned.1.call-done = bf16[64,8]{1,0:T(8,128)(2,1)} async-done(((bf16[1024,8]{1,0:T(8,128)(2,1)}), bf16[64,8]{1,0:T(8,128)(2,1)}) %reduce-scatter.29.cloned.1.call-update) | async-done | bytes 1040
  985.1 4.9 all-reduce.1
  991.2 57.7 %all-reduce.5.cloned.1.call-done = (bf16[64,4096]{1,0:T(8,128)(2,1)}, bf16[64,3072]{1,0:T(8,128)(2,1)}, bf16[64,1024]{1,0:T(8,128)(2,1)}, bf16[64,4096]{1,0:T(8,128)(2,1)}, bf16[256,1024]{1,0:T(8,128)(2,1)}) async-done(((bf16[64,4096]{1,0:T(8,128)(2,1)}, bf16[64,3072]{1,0:T(8,128)(2,1)}, bf16[64,1024]{1,0:T(8,128)(2,1)}, bf16[64,4096]{1,0:T(8,128)(2,1)}, bf16[256,1024]{1,0:T(8,128)(2,1)}), ...) | async-done | bytes 2097168 | tf_op jit(solution)/shard_map/psum | solution.py:243
  1048.8 1.7 convert_element_type.232
  1050.5 2.2 convert_element_type.226
  1052.8 1.9 convert_element_type.230
  1054.7 1.0 convert_element_type.234
  1055.7 1.1 convert_element_type.236
  (129 shorter events, 9.5 us)
Async XLA Ops:
  7.2 242.2 %copy-start = (bf16[1024,1024]{1,0:T(8,128)(2,1)S(1)}, bf16[1024,1024]{1,0:T(8,128)(2,1)}, u32[]{:S(2)}) copy-start(bf16[1024,1024]{1,0:T(8,128)(2,1)} %param.19) | copy-start | bytes 6291460
  7.2 4.4 copy-start.25
  7.2 59.3 %all-gather.8.cloned.1.call-start = ((), (), s32[]{:S(2)}) async-start(), calls=%async_computation.10 | async-start | bytes 3932160 | tf_op jit(solution)/shard_map/all_gather | solution.py:156
  9.6 8.1 copy-start.21
  9.6 8.1 slice-start.2
  11.6 6.1 copy-start.26
  11.7 5.9 copy-start.19
  11.8 5.9 copy-start.28
  11.8 5.9 copy-start.4
  11.8 5.9 slice-start.3
  17.7 4.9 copy-start.23
  17.7 4.9 copy-start.29
  24.6 1.3 copy-start.7
  24.6 82.4 %all-gather.6.cloned.1.call-start = ((), (), s32[]{:S(2)}) async-start(), calls=%async_computation.9 | async-start | bytes 3932160 | tf_op jit(solution)/shard_map/all_gather | solution.py:155
  25.4 151.8 %all-gather.4.cloned.1.call-start = ((), (), s32[]{:S(2)}) async-start(), calls=%async_computation.8 | async-start | bytes 7864320 | tf_op jit(solution)/shard_map/all_gather | solution.py:103
  29.0 429.1 %reduce-scatter.27.cloned.1.call-start = ((), (), s32[]{:S(2)}) async-start(), calls=%async_computation.17 | async-start | bytes 3932160
  31.8 159.7 %copy-start.2 = (bf16[1,640,1024]{1,2,0:T(8,128)(2,1)}, bf16[1,640,1024]{1,2,0:T(8,128)(2,1)S(1)}, u32[]{:S(2)}) copy-start(bf16[1,640,1024]{1,2,0:T(8,128)(2,1)S(1)} %copy.39) | copy-start | bytes 3932164
  211.5 17.3 %copy-start.12 = (bf16[1,1280,1024]{1,2,0:T(8,128)(2,1)S(1)}, bf16[1,1280,1024]{1,2,0:T(8,128)(2,1)}, u32[]{:S(2)}) copy-start(bf16[1,1280,1024]{1,2,0:T(8,128)(2,1)} %copy.38) | copy-start | bytes 7864324
  228.8 20.5 %copy-start.5 = (bf16[1,640,1024]{2,1,0:T(8,128)(2,1)S(1)}, bf16[1,640,1024]{2,1,0:T(8,128)(2,1)}, u32[]{:S(2)}) copy-start(bf16[1,640,1024]{2,1,0:T(8,128)(2,1)} %param.11) | copy-start | bytes 3932164
  249.3 1.7 copy-start.31
  251.0 47.7 %copy-start.10 = (f32[1,640,1024]{2,1,0:T(8,128)}, f32[1,640,1024]{2,1,0:T(8,128)S(1)}, u32[]{:S(2)}) copy-start(f32[1,640,1024]{2,1,0:T(8,128)S(1)} %get-tuple-element.38) | copy-start | bytes 7864324
  251.5 24.7 %copy-start.15 = (bf16[1,640,1024]{2,1,0:T(8,128)(2,1)S(1)}, bf16[1,640,1024]{2,1,0:T(8,128)(2,1)}, u32[]{:S(2)}) copy-start(bf16[1,640,1024]{2,1,0:T(8,128)(2,1)} %param.12) | copy-start | bytes 3932164
  251.5 38.4 %slice-start = ((s8[8388608]{0:T(1024)(128)(4,1)}), s8[4194304]{0:T(1024)(128)(4,1)S(1)}, s32[]{:S(2)}) async-start(s8[8388608]{0:T(1024)(128)(4,1)} %bitcast.215), calls=%async_computation.20 | async-start | bytes 8388608
  276.1 13.8 %slice-start.1 = ((s8[8388608]{0:T(1024)(128)(4,1)}), s8[4194304]{0:T(1024)(128)(4,1)S(1)}, s32[]{:S(2)}) async-start(s8[8388608]{0:T(1024)(128)(4,1)} %bitcast.215), calls=%async_computation.21 | async-start | bytes 8388608
  299.7 1.5 copy-start.9
  303.6 23.3 %copy-start.13 = (bf16[640,1024]{0,1:T(8,128)(2,1)}, bf16[640,1024]{0,1:T(8,128)(2,1)S(1)}, u32[]{:S(2)}) copy-start(bf16[640,1024]{0,1:T(8,128)(2,1)S(1)} %copy.42) | copy-start | bytes 3932164
  343.6 124.9 %reduce-scatter.25.cloned.1.call-start = ((), (), s32[]{:S(2)}) async-start(), calls=%async_computation.16 | async-start | bytes 3932160
  343.6 3.3 copy-start.11
  343.6 3.7 copy-start.14
  347.3 34.2 %copy-start.3 = (bf16[1,640,1024]{1,2,0:T(8,128)(2,1)S(1)}, bf16[1,640,1024]{1,2,0:T(8,128)(2,1)}, u32[]{:S(2)}) copy-start(bf16[1,640,1024]{1,2,0:T(8,128)(2,1)} %copy-done.2) | copy-start | bytes 3932164
  412.7 1.3 copy-start.32
  412.7 103.5 %reduce-scatter.19.cloned.1.call-start = ((), (), s32[]{:S(2)}) async-start(), calls=%async_computation.13 | async-start | bytes 2228224 | tf_op jit(solution)/shard_map/reduce_scatter | solution.py:231
  418.9 203.6 %reduce-scatter.21.cloned.1.call-start = ((), (), s32[]{:S(2)}) async-start(), calls=%async_computation.14 | async-start | bytes 8912896 | tf_op jit(solution)/shard_map/reduce_scatter | solution.py:234
  431.1 1.3 copy-start.16
  431.1 298.4 %reduce-scatter.23.cloned.1.call-start = ((), (), s32[]{:S(2)}) async-start(), calls=%async_computation.15 | async-start | bytes 8912896 | tf_op jit(solution)/shard_map/reduce_scatter | solution.py:237
  443.9 374.3 %reduce-scatter.17.cloned.1.call-start = ((), (), s32[]{:S(2)}) async-start(), calls=%async_computation.12 | async-start | bytes 6684672 | tf_op jit(solution)/shard_map/reduce_scatter | solution.py:228
  472.7 6.2 copy-start.6
  472.7 6.2 copy-start.22
  472.7 6.2 copy-start.24
  472.7 6.3 copy-start.27
  472.7 6.3 copy-start.30
  488.9 435.9 %reduce-scatter.15.cloned.1.call-start = ((), (), s32[]{:S(2)}) async-start(), calls=%async_computation.11 | async-start | bytes 8912896 | tf_op jit(solution)/shard_map/reduce_scatter | solution.py:222
  497.8 1.5 copy-start.8
  497.8 1.9 copy-start.20
  504.9 479.4 %reduce-scatter.29.cloned.1.call-start = ((), (), s32[]{:S(2)}) async-start(), calls=%async_computation.18 | async-start | bytes 278528
  505.0 9.9 copy-start.33
  514.9 533.9 %all-reduce.5.cloned.1.call-start = ((), (), s32[]{:S(2)}) async-start(), calls=%async_computation.19 | async-start | bytes 4194304 | tf_op jit(solution)/shard_map/psum | solution.py:243
  1048.8 5.9 copy-start.18
  1048.8 6.9 copy-start.17
  1050.5 6.3 copy-start.1
Sparse Core Ops, SparseCore 0:
  24.7 41.7 all-gather.7
  68.0 38.9 all-gather.5
  108.6 68.5 all-gather.3
  343.7 37.6 reduce-scatter.26
  412.8 37.6 reduce-scatter.24
  454.1 61.7 reduce-scatter.18
  520.0 102.3 reduce-scatter.20
  626.5 103.0 reduce-scatter.22
  733.5 84.6 reduce-scatter.16
  822.2 102.5 reduce-scatter.14
  928.9 55.3 reduce-scatter.28
  986.7 62.0 all-reduce.4
